TPU v7x, 768 devices: a whole 4x8x12 slice. The times are simulated.
768 devices in a mesh: dp: 16 (over y_hi, x), tensor: 48 (over z, y_lo, core).
Axes of the slice: x: 4, y: 8 (y_hi: 4, y_lo: 2; y = y_hi * 2 + y_lo), z: 12, core: 2. Of those that a mesh axis runs over, the one named last changes fastest.
Arguments:
- query_latent: bfloat16 [2, 6912, 1536], P(None, 'dp'), may hold values from -21 to 21
- key_latent: bfloat16 [2, 6912, 576], P(None, 'dp'), may hold values from -21 to 21
- partner: int32 [2, 48], replicated, may hold values from 0 to 47, as said below
- doc_length: int32 [2, 144], replicated, may hold values from 0 to 48, as said below
- up_query: bfloat16 [1536, 12288], P(None, 'tensor'), may hold values from -0.15625 to 0.15625
- up_rope: bfloat16 [1536, 6144], P(None, 'tensor'), may hold values from -0.15625 to 0.15625
- key_absorb: bfloat16 [12288, 512], P('tensor'), may hold values from -0.25 to 0.25
- value_expand: bfloat16 [512, 12288], P(None, 'tensor'), may hold values from -0.25 to 0.25
Outputs:
- head_out: bfloat16 [2, 6912, 12288], P(None, ('dp', 'tensor'))
Inputs may be any that keep to these rules, and one draw needn't show every extreme that they name: In each microbatch partner pairs the groups: partner[m, partner[m, g]] = g and partner[m, g] != g; of each pair one group is full and the other holds 1 to 2 documents; group g lies on dp index g // 3, and in each microbatch at least one pair joins groups whose dp indices are 8 apart. `doc_length`: live slots of a group come first, each with 12 to 48 tokens, the rest have length 0; the last 1 slots of a full group are 48 tokens long.
All inputs are finite; a program needn't handle non-finite values.
Results may differ from a plain program's by a relative error of at most 0.012.
The roundings to bfloat16 on the way count: a program that leaves them out, or rounds other values in their place, can miss the bound.
Values may be sent and summed in bfloat16 or wider, within the bound.
A program may use at most 64 MiB of HBM per device.

v0:
```python
import jax
import jax.numpy as jnp
from jax import lax
from jax.sharding import PartitionSpec as P

Q_RANK = 1536
KV_RANK = 512
ROPE = 64
NOPE = 128
V_HEAD = 128
DOC = 48
SLOTS = 3
SEND = 1
GROUP_DEV = 3


def rotation(row_count, half_width):
    position = (lax.iota(jnp.int32, row_count) % DOC).astype(jnp.float32)
    inverse_freq = 10000.0 ** (-lax.iota(jnp.float32, half_width) / half_width)
    angles = position[:, None] * inverse_freq[None, :]
    return (jnp.cos(angles), jnp.sin(angles))


def rotate(values, cosine, sine_part):
    half_width = values.shape[-1] // 2
    lower_half = values[..., :half_width]
    upper_half = values[..., half_width:]
    return jnp.concatenate(
        [
            lower_half * cosine - upper_half * sine_part,
            upper_half * cosine + lower_half * sine_part,
        ],
        -1,
    )


def attend(query_rows, key_rows, lengths, up_query, up_rope, key_absorb, value_expand):
    batches, row_count, _ = query_rows.shape
    head_count = key_absorb.shape[0] // NOPE
    blocks = row_count // DOC
    flat_rows = query_rows.reshape(batches * row_count, Q_RANK)
    query_nope = jnp.dot(flat_rows, up_query, preferred_element_type=jnp.float32).astype(
        jnp.bfloat16
    )
    query_nope = query_nope.reshape(batches * row_count, head_count, NOPE)
    absorb = key_absorb.reshape(head_count, NOPE, KV_RANK)
    absorbed = jnp.einsum(
        "rhd,hdc->rhc", query_nope, absorb, preferred_element_type=jnp.float32
    ).astype(jnp.bfloat16)
    cosine, sine_part = rotation(row_count, ROPE // 2)
    query_rope = jnp.dot(flat_rows, up_rope, preferred_element_type=jnp.float32).reshape(
        batches, row_count, head_count, ROPE
    )
    query_rope = rotate(query_rope, cosine[:, None, :], sine_part[:, None, :]).astype(jnp.bfloat16)
    latent = key_rows[..., :KV_RANK]
    key_rope = rotate(key_rows[..., KV_RANK:].astype(jnp.float32), cosine, sine_part).astype(
        jnp.bfloat16
    )
    queries = jnp.concatenate(
        [absorbed.reshape(batches, row_count, head_count, KV_RANK), query_rope], -1
    )
    queries = queries.reshape(batches, blocks, DOC, head_count, KV_RANK + ROPE)
    key_full = jnp.concatenate([latent, key_rope], -1).reshape(batches, blocks, DOC, KV_RANK + ROPE)
    scores = jnp.einsum("bnqhc,bnkc->bnhqk", queries, key_full, preferred_element_type=jnp.float32)
    scores = scores * (NOPE + ROPE) ** (-0.5)
    query_pos = lax.iota(jnp.int32, DOC)[:, None]
    key_pos = lax.iota(jnp.int32, DOC)[None, :]
    live_len = lengths[:, :, None, None, None]
    allowed = (key_pos <= query_pos) & ((key_pos < live_len) | (key_pos == query_pos))
    scores = jnp.where(allowed, scores, -jnp.inf)
    row_max = jnp.max(scores, -1, keepdims=True)
    weights = jnp.exp(scores - row_max)
    probability = (weights / jnp.sum(weights, -1, keepdims=True)).astype(jnp.bfloat16)
    latent_blocks = latent.reshape(batches, blocks, DOC, KV_RANK)
    mixed_latent = jnp.einsum(
        "bnhqk,bnkc->bnqhc", probability, latent_blocks, preferred_element_type=jnp.float32
    ).astype(jnp.bfloat16)
    expand = value_expand.reshape(KV_RANK, head_count, V_HEAD)
    result = jnp.einsum(
        "bnqhc,chv->bnqhv", mixed_latent, expand, preferred_element_type=jnp.float32
    )
    live_rows = lax.iota(jnp.int32, DOC)[None, None, :] < lengths[:, :, None]
    result = jnp.where(live_rows[:, :, :, None, None], result, 0.0).astype(jnp.bfloat16)
    return result.reshape(batches, row_count, head_count * V_HEAD)


def body(
    query_latent, key_latent, partner, doc_length, up_query, up_rope, key_absorb, value_expand
):
    micro_count = query_latent.shape[0]
    devices_dp = lax.axis_size("dp")
    groups = GROUP_DEV * devices_dp
    ranks = lax.axis_size("tensor")
    my_device = lax.axis_index("dp")
    my_rank = lax.axis_index("tensor")
    group_rows = SLOTS * DOC
    length_table = doc_length.reshape(micro_count, groups, SLOTS)
    counts = jnp.sum((length_table > 0).astype(jnp.int32), 2)
    my_groups = my_device * GROUP_DEV + lax.iota(jnp.int32, GROUP_DEV)
    own_hot = (lax.iota(jnp.int32, groups)[None, :] == my_groups[:, None])[None, :, :]
    own_length = jnp.sum(jnp.where(own_hot[:, :, :, None], length_table[:, None, :, :], 0), 2)
    own_count = jnp.sum(jnp.where(own_hot, counts[:, None, :], 0), 2)
    mate_index = jnp.sum(jnp.where(own_hot, partner[:, None, :], 0), 2)
    mate_hot = lax.iota(jnp.int32, groups)[None, None, :] == mate_index[:, :, None]
    mate_length = jnp.sum(jnp.where(mate_hot[:, :, :, None], length_table[:, None, :, :], 0), 2)
    is_heavy = own_count == SLOTS
    slot_sent = (lax.iota(jnp.int32, SLOTS) >= SLOTS - SEND)[None, None, :]
    mate_start = (SLOTS - SEND) * DOC
    share = SEND * DOC // ranks
    share_start = mate_start + my_rank * share
    query_groups = query_latent.reshape(micro_count, GROUP_DEV, group_rows, Q_RANK)
    key_groups = key_latent.reshape(micro_count, GROUP_DEV, group_rows, KV_RANK + ROPE)
    query_share = lax.dynamic_slice_in_dim(query_groups, share_start, share, 2)
    key_share = lax.dynamic_slice_in_dim(key_groups, share_start, share, 2)
    zero_half = jnp.zeros((), jnp.bfloat16)
    routed = (mate_hot & is_heavy[:, :, None]).reshape(
        micro_count, GROUP_DEV, devices_dp, GROUP_DEV
    )
    routed = jnp.transpose(routed, (2, 0, 3, 1))[:, :, :, :, None, None]
    query_out = jnp.sum(
        jnp.where(routed, query_share[None, :, None], zero_half).astype(jnp.float32), 3
    ).astype(jnp.bfloat16)
    key_out = jnp.sum(
        jnp.where(routed, key_share[None, :, None], zero_half).astype(jnp.float32), 3
    ).astype(jnp.bfloat16)
    query_in, key_in = (
        lax.all_to_all(query_out, "dp", split_axis=0, concat_axis=0, tiled=True),
        lax.all_to_all(key_out, "dp", split_axis=0, concat_axis=0, tiled=True),
    )
    query_recv = jnp.sum(query_in.astype(jnp.float32), 0).astype(jnp.bfloat16)
    key_recv = jnp.sum(key_in.astype(jnp.float32), 0).astype(jnp.bfloat16)
    query_mate, key_mate = (
        lax.all_gather(query_recv, "tensor", axis=2, tiled=True),
        lax.all_gather(key_recv, "tensor", axis=2, tiled=True),
    )
    batch_count = micro_count * GROUP_DEV
    own_lengths = jnp.where(slot_sent & is_heavy[:, :, None], 0, own_length)
    far_lengths = jnp.where(is_heavy[:, :, None], 0, mate_length[:, :, SLOTS - SEND :])
    own_out = attend(
        query_groups.reshape(batch_count, group_rows, Q_RANK),
        key_groups.reshape(batch_count, group_rows, KV_RANK + ROPE),
        own_lengths.reshape(batch_count, SLOTS),
        up_query,
        up_rope,
        key_absorb,
        value_expand,
    )
    mate_out = attend(
        query_mate.reshape(batch_count, SEND * DOC, Q_RANK),
        key_mate.reshape(batch_count, SEND * DOC, KV_RANK + ROPE),
        far_lengths.reshape(batch_count, SEND),
        up_query,
        up_rope,
        key_absorb,
        value_expand,
    )
    produced = own_out + jnp.pad(mate_out, ((0, 0), (mate_start, 0), (0, 0)))
    produced = produced.reshape(micro_count, GROUP_DEV * group_rows, produced.shape[-1])
    return lax.all_to_all(produced, "tensor", split_axis=1, concat_axis=2, tiled=True)


def solution(mesh):
    in_specs = (
        P(None, "dp", None),
        P(None, "dp", None),
        P(),
        P(),
        P(None, "tensor"),
        P(None, "tensor"),
        P("tensor", None),
        P(None, "tensor"),
    )
    out_specs = P(None, ("dp", "tensor"), None)
    return jax.shard_map(body, mesh=mesh, in_specs=in_specs, out_specs=out_specs, check_vma=False)
```

profile of v0, /device:TPU:17, one launch (start us, length us, event | category | flops | bytes accessed | tf_op | source)
XLA Modules:
  0.0 388.4 jit_solution(10000459589453727095)
XLA Ops:
  0.1 0.9 reshape.561
  1.1 0.1 convert_reduce_fusion
  1.2 0.9 select_reduce_fusion.4
  2.1 0.1 copy.119
  2.3 0.9 constant_dynamic-slice_fusion
  3.2 0.1 select_reduce_fusion.1
  3.4 0.8 copy.140
  4.1 9.3 %all-to-all-start = ((bf16[16,2,3,1,576]{4,1,3,2,0:T(2,128)(2,1)}), bf16[16,2,3,1,576]{4,1,3,2,0:T(2,128)(2,1)}, u32[]{:S(2)}, u32[]{:S(2)}) async-start(bf16[16,2,3,1,576]{4,1,3,2,0:T(2,128)(2,1)} %copy.140), calls=%async_computation | async-start | bytes 245760 | tf_op jit(solution)/shard_map/all_to_all | solution.py:128
  13.8 1.0 slice_convert_fusion
  14.7 2.1 slice.52
  17.0 0.2 select_reduce_fusion
  17.2 1.0 copy.145
  18.2 0.9 copy.126
  19.1 0.4 select_reduce_fusion.2
  19.7 0.7 iota_compare_fusion.3
  20.3 1.7 reshape.566
  22.1 0.1 copy.121
  22.3 0.1 copy.122
  22.5 0.8 multiply_cosine_fusion.1
  23.3 0.2 multiply_cosine_fusion
  23.5 0.7 copy.123
  24.2 0.7 copy.124
  25.0 1.9 fusion.72
  26.8 0.9 subtract_convert_fusion.1
  27.7 1.1 concatenate.34
  28.8 1.0 copy.128
  29.8 1.1 concatenate.35
  31.0 1.0 copy.129
  32.0 2.0 fusion.30
  34.1 1.8 convolution_convert_fusion
  35.9 0.8 or_and_fusion
  36.7 0.2 subtract_convert_fusion
  36.9 1.2 pad_maximum_fusion
  38.1 5.3 %fusion.68 = (f32[6,3,2,48]{3,2,1,0:T(2,128)}, f32[6,3,2,48,48]{3,4,2,1,0:T(8,128)}) fusion(bf16[6,3,48,576,1]{3,2,4,1,0:T(8,128)(2,1)} %bitcast.152, bf16[6,3,48,2,32]{4,2,3,1,0:T(8,128)(2,1)} %copy.129, bf16[6,3,48,2,32]{4,2,3,1,0:T(8,128)(2,1)} %copy.128, pred[6,3,48,48]{2,3,1,0:T(8,128)(4,1)} %or_and_fusion, bf16[6,3,48,2,512]{4,2,1,0,3:T(8,128)(2,1)} %bitcast.145), kind=kOutput, calls=%fused_computation.110 | convolution fusion | flops 101855280 | bytes 3366144 | tf_op jit(solution)/shard_map/sub | solution.py:72
  43.4 3.1 fusion.31
  46.5 1.4 copy.132
  47.9 1.0 reshape.567
  48.9 0.7 or_and_fusion.1
  49.7 9.1 %all-to-all-start.1 = ((bf16[16,2,3,1,1536]{4,1,3,2,0:T(2,128)(2,1)}), bf16[16,2,3,1,1536]{4,1,3,2,0:T(2,128)(2,1)}, u32[]{:S(2)}, u32[]{:S(2)}) async-start(bf16[16,2,3,1,1536]{4,1,3,2,0:T(2,128)(2,1)} %copy.145), calls=%async_computation.1 | async-start | bytes 589824 | tf_op jit(solution)/shard_map/all_to_all | solution.py:127
  58.7 1.0 reduce_sum.130
  59.8 0.2 copy.141
  60.0 204.3 %all-gather = bf16[2,3,27648]{1,0,2:T(2,128)(2,1)} all-gather(bf16[2,3,576]{1,0,2:T(2,128)(2,1)S(1)} %copy.141), channel_id=2, replica_groups=mesh['dp'=16,'tensor'=48] {'tensor'}, dimensions={2}, use_global_device_ids=true | all-gather | bytes 338688 | tf_op jit(solution)/shard_map/all_gather | solution.py:134
  264.4 27.7 %copy.142 = bf16[2,3,27648]{2,1,0:T(4,128)(2,1)S(1)} copy(bf16[2,3,27648]{1,0,2:T(2,128)(2,1)} %all-gather) | data formatting | bytes 663552 | tf_op jit(solution)/shard_map/all_gather | solution.py:134
  292.1 0.4 reshape.569
  292.5 0.8 subtract_convert_fusion.3
  293.3 1.2 reduce_sum.134
  294.5 53.2 %all-gather.1 = bf16[2,3,73728]{2,0,1:T(2,128)(2,1)S(1)} all-gather(bf16[2,3,1536]{2,0,1:T(2,128)(2,1)S(1)} %reduce_sum.134), channel_id=3, replica_groups=mesh['dp'=16,'tensor'=48] {'tensor'}, dimensions={2}, use_global_device_ids=true | all-gather | bytes 903168 | tf_op jit(solution)/shard_map/all_gather | solution.py:133
  347.7 1.8 copy.146
  349.5 3.1 reshape.587
  352.6 2.3 reshape_reshape.7
  354.9 1.7 fusion.40
  356.7 1.0 subtract_convert_fusion.2
  357.7 0.4 fusion.39
  358.1 0.3 convolution_convert_fusion.2
  358.4 0.6 fusion.69
  359.2 0.2 copy-done.5
  359.4 0.4 fusion.26
  359.8 0.3 copy-done.12
  360.0 0.3 fusion.38
  360.4 0.1 copy.153
  360.5 0.1 reshape.575
  360.7 0.3 copy.154
  361.0 26.3 %all_to_all.28 = bf16[2,432,256]{2,0,1:T(2,128)(2,1)S(1)} all-to-all(bf16[2,432,256]{2,0,1:T(2,128)(2,1)S(1)} %copy.154), channel_id=1, replica_groups=mesh['dp'=16,'tensor'=48] {'tensor'}, dimensions={1} | all-to-all | bytes 884736 | tf_op jit(solution)/shard_map/all_to_all | solution.py:159
  387.3 1.1 copy.176
  (73 shorter events, 1.3 us)
Async XLA Ops:
  0.0 16.9 %copy-start = (bf16[2,432,1536]{2,1,0:T(8,128)(2,1)S(1)}, bf16[2,432,1536]{2,1,0:T(8,128)(2,1)}, u32[]{:S(2)}) copy-start(bf16[2,432,1536]{2,1,0:T(8,128)(2,1)} %param.8) | copy-start | bytes 7962628
  4.1 45.6 %all-to-all-start = ((bf16[16,2,3,1,576]{4,1,3,2,0:T(2,128)(2,1)}), bf16[16,2,3,1,576]{4,1,3,2,0:T(2,128)(2,1)}, u32[]{:S(2)}, u32[]{:S(2)}) async-start(bf16[16,2,3,1,576]{4,1,3,2,0:T(2,128)(2,1)} %copy.140), calls=%async_computation | async-start | bytes 245760 | tf_op jit(solution)/shard_map/all_to_all | solution.py:128
  13.7 4.5 %copy-start.9 = (bf16[1536,128]{1,0:T(8,128)(2,1)S(1)}, bf16[1536,128]{1,0:T(8,128)(2,1)}, u32[]{:S(2)}) copy-start(bf16[1536,128]{1,0:T(8,128)(2,1)} %param.13) | copy-start | bytes 1179652
  22.5 13.4 %copy-start.18 = (pred[6,3,48]{2,1,0:T(4,128)(4,1)}, pred[6,3,48]{2,1,0:T(4,128)(4,1)S(1)}, u32[]{:S(2)}) copy-start(pred[6,3,48]{2,1,0:T(4,128)(4,1)S(1)} %iota_compare_fusion.2) | copy-start | bytes 2596
  32.0 2.1 copy-start.6
  34.0 2.7 copy-start.10
  34.0 2.7 copy-start.11
  34.0 2.9 copy-start.1
  38.1 5.3 %copy-start.2 = (bf16[6,144,512]{2,1,0:T(8,128)(2,1)S(1)}, bf16[6,144,512]{2,1,0:T(8,128)(2,1)}, u32[]{:S(2)}) copy-start(bf16[6,144,512]{2,1,0:T(8,128)(2,1)} %slice.52) | copy-start | bytes 2654212
  46.5 2.4 copy-start.19
  49.7 243.6 %all-to-all-start.1 = ((bf16[16,2,3,1,1536]{4,1,3,2,0:T(2,128)(2,1)}), bf16[16,2,3,1,1536]{4,1,3,2,0:T(2,128)(2,1)}, u32[]{:S(2)}, u32[]{:S(2)}) async-start(bf16[16,2,3,1,1536]{4,1,3,2,0:T(2,128)(2,1)} %copy.145), calls=%async_computation.1 | async-start | bytes 589824 | tf_op jit(solution)/shard_map/all_to_all | solution.py:127
  264.4 28.2 %copy-start.13 = (f32[48,32]{1,0:T(8,128)S(1)}, f32[48,32]{1,0:T(8,128)}, u32[]{:S(2)}) copy-start(f32[48,32]{1,0:T(8,128)} %get-tuple-element.19) | copy-start | bytes 18436
  264.4 28.2 %copy-start.14 = (f32[48,32]{1,0:T(8,128)S(1)}, f32[48,32]{1,0:T(8,128)}, u32[]{:S(2)}) copy-start(f32[48,32]{1,0:T(8,128)} %get-tuple-element.20) | copy-start | bytes 18436
  292.5 57.0 %copy-start.4 = (bf16[6,48,576]{2,1,0:T(8,128)(2,1)}, bf16[6,48,576]{2,1,0:T(8,128)(2,1)S(1)}, u32[]{:S(2)}) copy-start(bf16[6,48,576]{2,1,0:T(8,128)(2,1)S(1)} %reshape.569) | copy-start | bytes 995332
  354.8 2.8 copy-start.8
  356.6 1.4 copy-start.7
  356.6 1.7 slice-start
  356.6 1.7 copy-start.15
  356.6 1.7 copy-start.16
  356.7 1.7 copy-start.17
  358.4 1.0 copy-start.5
  359.1 1.0 copy-start.12
  359.1 1.0 copy-start.20
  359.4 1.2 copy-start.3
where the time goes:
time: 390 us; the launch traced here: 388 us
  blocking collectives  284 us (73%)
  local copies, waits for them, and re-layouts  55.1 us (14%)
  starting transfers between devices  18.4 us (5%)
  matrix products  17.9 us (5%)
  other arithmetic  12.7 us (3%)
    all_gather x1, blocking collectives, body(): lax.all_gather(key_recv, 'tensor', axis=2, tiled=True)  204 us
    all_gather x1, blocking collectives, body(): lax.all_gather(query_recv, 'tensor', axis=2, tiled=True)  53.2 us
    all_gather x1, local copies, waits for them, and re-layouts, body(): lax.all_gather(key_recv, 'tensor', axis=2, tiled=True)  27.7 us
    all_to_all x1, blocking collectives, body(): lax.all_to_all(produced, 'tensor', split_axis=1, concat_axis=2, tiled=True)  26.3 us
    all_to_all x1, starting transfers between devices, body(): lax.all_to_all(key_out, 'dp', split_axis=0, concat_axis=0, tiled=True)  9.35 us
    all_to_all x1, starting transfers between devices, body(): lax.all_to_all(query_out, 'dp', split_axis=0, concat_axis=0, tiled=True)  9.06 us
  transfers between devices with their start and end apart: 2, of which 0 were waited for; matrix products, arithmetic and copies ran while one was open for 17% of the time, Pallas kernels for 0%

commit v1 on v0

v1 whole, which is shorter than its diff:
```python
import functools

import jax
import jax.numpy as jnp
import numpy as np
from jax import lax
from jax.experimental import pallas as pl
from jax.experimental.pallas import tpu as pltpu
from jax.sharding import PartitionSpec as P

Q_RANK = 1536
KV_RANK = 512
ROPE = 64
NOPE = 128
V_HEAD = 128
DOC = 48
SLOTS = 3
GROUP_DEV = 3
ROWS = SLOTS * DOC
MB = 2
MESH = pl.DeviceIdType.MESH
X_DEV = 4
Y_DEV = 4
RANKS = 48
OWN_ROWS = 9
CUT = 10
TAIL = CUT * OWN_ROWS


def rope_tables():
    freq = 10000.0 ** (-np.arange(32, dtype=np.float32) / np.float32(32))
    angles = np.arange(DOC, dtype=np.float32)[:, None] * freq.astype(np.float32)[None, :]
    cosine = np.cos(angles.astype(np.float64)).astype(np.float32)
    sine = np.sin(angles.astype(np.float64)).astype(np.float32)
    cos_row = np.concatenate([cosine] * 4, 1)
    sin_row = np.concatenate([-sine, sine, -sine, sine], 1)
    return np.stack([cos_row, sin_row])


def dot(a, b, dims=((1,), (0,))):
    return lax.dot_general(a, b, (dims, ((), ())), preferred_element_type=jnp.float32)


def rotate_pairs(values, cosine, sine):
    lane = lax.broadcasted_iota(jnp.int32, values.shape, 1)
    swapped = jnp.where(
        lane % 64 < 32, pltpu.roll(values, 96, 1), pltpu.roll(values, 32, 1)
    )
    return values * cosine + swapped * sine


def compute_kernel(len_ref, q_ref, k_ref, uq_ref, ur_ref, ab_ref, ve_ref, tab_ref, o_ref, mix_ref):
    my_dp = lax.axis_index("dp")
    scale = (NOPE + ROPE) ** -0.5
    row_pos = lax.broadcasted_iota(jnp.int32, (2 * DOC, DOC), 0) % DOC
    key_pos = lax.broadcasted_iota(jnp.int32, (2 * DOC, DOC), 1)
    out_pos = lax.broadcasted_iota(jnp.int32, (DOC, 2 * V_HEAD), 0)
    lane = lax.broadcasted_iota(jnp.int32, (DOC, 128), 1)

    def group(b, carry):
        m = b // GROUP_DEV
        j = b % GROUP_DEV
        rows = pl.ds(pl.multiple_of(j * ROWS, ROWS), ROWS)
        x = q_ref[m, rows, :]
        nope = dot(x, uq_ref[...]).astype(jnp.bfloat16)
        rope = dot(x, ur_ref[...])
        absorbed = [
            dot(nope[:, h * NOPE : (h + 1) * NOPE], ab_ref[h * NOPE : (h + 1) * NOPE, :]).astype(
                jnp.bfloat16
            )
            for h in range(2)
        ]
        for s in range(SLOTS):
            lo, hi = s * DOC, (s + 1) * DOC
            here = pl.ds(pl.multiple_of(j * ROWS + s * DOC, DOC), DOC)
            latent = k_ref[m, here, 0:KV_RANK]
            kr = k_ref[m, here, KV_RANK : KV_RANK + ROPE].astype(jnp.float32)
            kr = jnp.concatenate([kr, kr], 1)
            kr = rotate_pairs(kr, tab_ref[0], tab_ref[1]).astype(jnp.bfloat16)
            qr = rotate_pairs(rope[lo:hi], tab_ref[0], tab_ref[1])
            qr = jnp.concatenate(
                [jnp.where(lane < 64, qr, 0.0), jnp.where(lane < 64, 0.0, qr)], 0
            ).astype(jnp.bfloat16)
            qa = jnp.concatenate([absorbed[0][lo:hi], absorbed[1][lo:hi]], 0)
            scores = dot(qa, latent, ((1,), (1,))) + dot(qr, kr, ((1,), (1,)))
            length = len_ref[m, (my_dp * GROUP_DEV + j) * SLOTS + s]
            allowed = (key_pos <= row_pos) & ((key_pos < length) | (key_pos == row_pos))
            scores = jnp.where(allowed, scores * scale, -jnp.inf)
            weights = jnp.exp(scores - jnp.max(scores, 1, keepdims=True))
            prob = (weights / jnp.sum(weights, 1, keepdims=True)).astype(jnp.bfloat16)
            mixed = dot(prob, latent).astype(jnp.bfloat16)
            mix_ref[0, lo:hi, :] = mixed[:DOC]
            mix_ref[1, lo:hi, :] = mixed[DOC:]
        for h in range(2):
            res = dot(mix_ref[h], ve_ref[:, h * V_HEAD : (h + 1) * V_HEAD])
            for s in range(SLOTS):
                here = pl.ds(pl.multiple_of(j * ROWS + s * DOC, DOC), DOC)
                length = len_ref[m, (my_dp * GROUP_DEV + j) * SLOTS + s]
                part = jnp.where(out_pos[:, :V_HEAD] < length, res[s * DOC : (s + 1) * DOC], 0.0)
                o_ref[m, here, h * V_HEAD : (h + 1) * V_HEAD] = part.astype(jnp.bfloat16)
        return carry

    lax.fori_loop(0, MB * GROUP_DEV, group, 0)


def compute(doc_length, query, key, up_query, up_rope, key_absorb, value_expand):
    vm = pl.BlockSpec(memory_space=pltpu.VMEM)
    return pl.pallas_call(
        compute_kernel,
        out_shape=jax.ShapeDtypeStruct((MB, GROUP_DEV * ROWS, 2 * V_HEAD), jnp.bfloat16),
        in_specs=[pl.BlockSpec(memory_space=pltpu.SMEM)] + [vm] * 7,
        out_specs=vm,
        scratch_shapes=[pltpu.VMEM((2, ROWS, KV_RANK), jnp.bfloat16)],
        name="attend",
    )(doc_length, query, key, up_query, up_rope, key_absorb, value_expand, jnp.asarray(rope_tables()))


def comm_kernel(
    partner_ref,
    len_ref,
    in_ref,
    out_ref,
    recv1,
    snd2,
    recv2,
    merged,
    local_sem,
    y_send,
    y_recv,
    x_send,
    x_recv,
    t_send,
    t_recv,
):
    me_dp = lax.axis_index("dp")
    me_t = lax.axis_index("tensor")
    me_x = me_dp % X_DEV
    me_y = me_dp // X_DEV

    def y_peer(step):
        return lax.rem(me_y + step, Y_DEV) * X_DEV + me_x

    def x_peer(step):
        return me_y * X_DEV + lax.rem(me_x + step, X_DEV)

    barrier = pltpu.get_barrier_semaphore()
    for step in range(1, Y_DEV):
        pl.semaphore_signal(
            barrier, inc=1, device_id={"dp": y_peer(step), "tensor": me_t}, device_id_type=MESH
        )
    for step in range(1, X_DEV):
        pl.semaphore_signal(
            barrier, inc=1, device_id={"dp": x_peer(step), "tensor": me_t}, device_id_type=MESH
        )

    def greet(step, carry):
        pl.semaphore_signal(
            barrier,
            inc=1,
            device_id={"dp": me_dp, "tensor": lax.rem(me_t + step, RANKS)},
            device_id_type=MESH,
        )
        return carry

    lax.fori_loop(1, RANKS, greet, 0)
    tail_copy = pltpu.make_async_copy(
        in_ref.at[:, pl.ds(TAIL, SLOTS * DOC - DOC - TAIL)],
        merged.at[:, pl.ds(0, SLOTS * DOC - DOC - TAIL)],
        local_sem.at[0],
    )
    tail_copy.start()
    docs = in_ref.at[:, pl.ds((SLOTS - 1) * DOC, DOC)]
    own_copy = pltpu.make_async_copy(docs, recv1.at[me_y], local_sem.at[1])
    own_copy.start()
    pl.semaphore_wait(barrier, RANKS - 1 + X_DEV - 1 + Y_DEV - 1)

    def y_copy(step):
        return pltpu.make_async_remote_copy(
            src_ref=docs,
            dst_ref=recv1.at[me_y],
            send_sem=y_send.at[step - 1],
            recv_sem=y_recv.at[step - 1],
            device_id={"dp": y_peer(step), "tensor": me_t},
            device_id_type=MESH,
        )

    for step in (2, 1, 3):
        y_copy(step).start()

    def t_copy(rank, source):
        return pltpu.make_async_remote_copy(
            src_ref=source,
            dst_ref=out_ref.at[:, :, pl.ds(pl.multiple_of(me_t * 256, 256), 256)],
            send_sem=t_send.at[rank],
            recv_sem=t_recv.at[me_t],
            device_id={"dp": me_dp, "tensor": rank},
            device_id_type=MESH,
        )

    def self_copy(source):
        return pltpu.make_async_copy(
            source,
            out_ref.at[:, :, pl.ds(pl.multiple_of(me_t * 256, 256), 256)],
            local_sem.at[2],
        )

    def first_source(rank):
        return in_ref.at[rank // 16, pl.ds((rank % 16) * OWN_ROWS, OWN_ROWS)]

    def second_source(rank):
        return merged.at[rank // 16, pl.ds((rank % 16 - CUT) * OWN_ROWS, OWN_ROWS)]

    def send_first(step, carry):
        rank = lax.rem(me_t + step, RANKS)

        @pl.when(rank % 16 < CUT)
        def _():
            t_copy(rank, first_source(rank)).start()

        return carry

    lax.fori_loop(1, RANKS, send_first, 0)

    @pl.when(me_t % 16 < CUT)
    def _():
        self_copy(first_source(me_t)).start()

    own_copy.wait()
    tail_copy.wait()
    for step in range(1, Y_DEV):
        y_copy(step).wait_recv()

    micro = lax.broadcasted_iota(jnp.int32, (DOC, MB, 2 * V_HEAD), 1)

    def wanted(x_at, j, m):
        return partner_ref[m, (me_y * X_DEV + x_at) * GROUP_DEV + j]

    for step in range(X_DEV):
        x_at = lax.rem(me_x + step, X_DEV)
        for j in range(GROUP_DEV):
            first = wanted(x_at, j, 0)
            second = wanted(x_at, j, 1)
            a = recv1[first // (X_DEV * GROUP_DEV), first % GROUP_DEV]
            b = recv1[second // (X_DEV * GROUP_DEV), second % GROUP_DEV]
            picked = jnp.where(micro == 0, a, b)
            if step == 0:
                recv2[me_x, j] = picked
            else:
                snd2[step - 1, j] = picked

    def x_copy(step):
        return pltpu.make_async_remote_copy(
            src_ref=snd2.at[step - 1],
            dst_ref=recv2.at[me_x],
            send_sem=x_send.at[step - 1],
            recv_sem=x_recv.at[step - 1],
            device_id={"dp": x_peer(step), "tensor": me_t},
            device_id_type=MESH,
        )

    for step in (2, 1, 3):
        x_copy(step).start()
    for step in range(1, X_DEV):
        x_copy(step).wait_recv()

    for j in range(GROUP_DEV):
        picks = []
        for m in range(MB):
            group = me_dp * GROUP_DEV + j
            source_x = (partner_ref[m, group] // GROUP_DEV) % X_DEV
            live = jnp.int32(0)
            for s in range(SLOTS):
                live += (len_ref[m, group * SLOTS + s] > 0).astype(jnp.int32)
            value = recv2[source_x, j]
            picks.append(jnp.where(live < SLOTS, value, jnp.zeros_like(value)))
        merged[j, pl.ds(SLOTS * DOC - DOC - TAIL, DOC)] = jnp.where(micro == 0, picks[0], picks[1])

    def send_second(step, carry):
        rank = lax.rem(me_t + step, RANKS)

        @pl.when(rank % 16 >= CUT)
        def _():
            t_copy(rank, second_source(rank)).start()

        return carry

    lax.fori_loop(1, RANKS, send_second, 0)

    @pl.when(me_t % 16 >= CUT)
    def _():
        self_copy(second_source(me_t)).start()

    def finish(step, carry):
        source = lax.rem(me_t + step, RANKS)
        pltpu.make_async_remote_copy(
            src_ref=merged.at[0, pl.ds(0, OWN_ROWS)],
            dst_ref=out_ref.at[:, :, pl.ds(pl.multiple_of(source * 256, 256), 256)],
            send_sem=t_send.at[source],
            recv_sem=t_recv.at[source],
            device_id={"dp": me_dp, "tensor": source},
            device_id_type=MESH,
        ).wait()
        return carry

    lax.fori_loop(1, RANKS, finish, 0)
    self_copy(merged.at[0, pl.ds(0, OWN_ROWS)]).wait()
    for step in range(1, Y_DEV):
        y_copy(step).wait_send()
    for step in range(1, X_DEV):
        x_copy(step).wait_send()


def exchange(partner, doc_length, produced):
    docs = (GROUP_DEV, DOC, MB, 2 * V_HEAD)
    smem = pl.BlockSpec(memory_space=pltpu.SMEM)
    vm = pl.BlockSpec(memory_space=pltpu.VMEM)
    return pl.pallas_call(
        comm_kernel,
        out_shape=jax.ShapeDtypeStruct((OWN_ROWS, MB, RANKS * 2 * V_HEAD), jnp.bfloat16),
        in_specs=[smem, smem, vm],
        out_specs=vm,
        scratch_shapes=[
            pltpu.VMEM((Y_DEV,) + docs, jnp.bfloat16),
            pltpu.VMEM((X_DEV - 1,) + docs, jnp.bfloat16),
            pltpu.VMEM((X_DEV,) + docs, jnp.bfloat16),
            pltpu.VMEM((GROUP_DEV, ROWS - TAIL, MB, 2 * V_HEAD), jnp.bfloat16),
            pltpu.SemaphoreType.DMA((3,)),
            pltpu.SemaphoreType.DMA((Y_DEV - 1,)),
            pltpu.SemaphoreType.DMA((Y_DEV - 1,)),
            pltpu.SemaphoreType.DMA((X_DEV - 1,)),
            pltpu.SemaphoreType.DMA((X_DEV - 1,)),
            pltpu.SemaphoreType.DMA((RANKS,)),
            pltpu.SemaphoreType.DMA((RANKS,)),
        ],
        compiler_params=pltpu.CompilerParams(collective_id=0, has_side_effects=True),
        name="exchange",
    )(partner, doc_length, produced)


def body(
    query_latent, key_latent, partner, doc_length, up_query, up_rope, key_absorb, value_expand
):
    produced = compute(
        doc_length, query_latent, key_latent, up_query, up_rope, key_absorb, value_expand
    )
    produced = produced.reshape(MB, GROUP_DEV, ROWS, 2 * V_HEAD).transpose(1, 2, 0, 3)
    result = exchange(partner, doc_length, produced)
    return result.transpose(1, 0, 2)


def solution(mesh):
    in_specs = (
        P(None, "dp", None),
        P(None, "dp", None),
        P(),
        P(),
        P(None, "tensor"),
        P(None, "tensor"),
        P("tensor", None),
        P(None, "tensor"),
    )
    out_specs = P(None, ("dp", "tensor"), None)
    return jax.shard_map(body, mesh=mesh, in_specs=in_specs, out_specs=out_specs, check_vma=False)
```

time: 390 us -> 76.9 us (0.20)
  the two profiles are of different devices: /device:TPU:17 before, /device:TPU:153 now
where the time goes in v1:
time: 76.9 us; the launch traced here: 76.7 us
  Pallas kernels  72.4 us (94%)
  local copies, waits for them, and re-layouts  4.24 us (6%)
    pallas_call x1, Pallas kernels, exchange(): pl.pallas_call(comm_kernel, out_shape=jax.ShapeDtypeStruct((OWN_ROWS, MB,...  58.1 us
    pallas_call x1, Pallas kernels, compute(): pl.pallas_call(compute_kernel, out_shape=jax.ShapeDtypeStruct((MB, GROUP_...  14.3 us
    pallas_call x1, local copies, waits for them, and re-layouts, compute(): pl.pallas_call(compute_kernel, out_shape=jax.ShapeDtypeStruct((MB, GROUP_...  2.12 us
    unnamed x1, local copies, waits for them, and re-layouts  2.11 us

profile of v1, /device:TPU:153, one launch (start us, length us, event | category | flops | bytes accessed | tf_op | source)
XLA Modules:
  0.0 76.7 jit_solution(14946397598674148220)
XLA Ops:
  0.0 14.3 %attend.1 = bf16[2,432,256]{2,1,0:T(8,128)(2,1)} custom-call(s32[2,144]{1,0:T(2,128)} %len_ref.3, bf16[2,432,1536]{2,1,0:T(8,128)(2,1)} %q_ref.1, bf16[2,432,576]{2,1,0:T(8,128)(2,1)} %k_ref.1, bf16[1536,256]{1,0:T(8,128)(2,1)} %uq_ref.1, bf16[1536,128]{1,0:T(8,128)(2,1)} %ur_ref.1, bf16[256,512]{1,0:T(8,128)(2,1)} %ab_ref.1, bf16[512,256]{1,0:T(8,128)(2,1)} %ve_ref.1, ...), custom_call_target="tpu_custom_call" | custom-call | tf_op jit(solution)/shard_map/attend/pallas_call | solution.py:108
  14.3 2.1 %copy.10 = bf16[2,432,256]{2,0,1:T(2,128)(2,1)} copy(bf16[2,432,256]{2,1,0:T(8,128)(2,1)} %attend.1) | data formatting | bytes 884736 | tf_op jit(solution)/shard_map/attend/pallas_call | solution.py:108
  16.4 58.1 %exchange.1 = bf16[9,2,12288]{2,1,0:T(2,128)(2,1)} custom-call(s32[2,48]{1,0:T(2,128)} %partner_ref.1, s32[2,144]{1,0:T(2,128)} %len_ref.3, bf16[3,144,2,256]{3,2,1,0:T(2,128)(2,1)} %bitcast.4), custom_call_target="tpu_custom_call" | custom-call | tf_op jit(solution)/shard_map/exchange/pallas_call | solution.py:317
  74.6 2.1 %copy.12 = bf16[2,9,12288]{2,0,1:T(2,128)(2,1)} copy(bf16[2,9,12288]{2,0,1:T(2,128)(2,1)} %bitcast.5) | data formatting | bytes 884736

commit v2 on v1

v2 whole, which is shorter than its diff:
```python
import jax
import jax.numpy as jnp
import numpy as np
from jax import lax
from jax.experimental import pallas as pl
from jax.experimental.pallas import tpu as pltpu
from jax.sharding import PartitionSpec as P

Q_RANK = 1536
KV_RANK = 512
ROPE = 64
NOPE = 128
V_HEAD = 128
DOC = 48
SLOTS = 3
GROUP_DEV = 3
ROWS = SLOTS * DOC
MB = 2
PAIR = MB * DOC
UNITS = GROUP_DEV * SLOTS
BLOCK = 3
MESH = pl.DeviceIdType.MESH
X_DEV = 4
Y_DEV = 4
RANKS = 48
OWN_ROWS = 9
SHARE = ROWS // OWN_ROWS
CUT = 10
TAIL = CUT * OWN_ROWS
HALF = (SLOTS - 1) * DOC - TAIL
CHUNKS = 3
CHUNK = PAIR // CHUNKS
BF16 = jnp.bfloat16


def rope_tables():
    freq = 10000.0 ** (-np.arange(32, dtype=np.float32) / np.float32(32))
    angles = np.arange(DOC, dtype=np.float32)[:, None] * freq.astype(np.float32)[None, :]
    cosine = np.cos(angles.astype(np.float64)).astype(np.float32)
    sine = np.sin(angles.astype(np.float64)).astype(np.float32)
    cos_row = np.concatenate([cosine] * 4, 1)
    sin_row = np.concatenate([-sine, sine, -sine, sine], 1)
    return np.stack([np.concatenate([t] * MB, 0) for t in (cos_row, sin_row)])


def dot(a, b, dims=((1,), (0,))):
    return lax.dot_general(a, b, (dims, ((), ())), preferred_element_type=jnp.float32)


def rotate_pairs(values, cosine, sine):
    lane = lax.broadcasted_iota(jnp.int32, values.shape, 1)
    swapped = jnp.where(
        lane % 64 < 32, pltpu.roll(values, 96, 1), pltpu.roll(values, 32, 1)
    )
    return values * cosine + swapped * sine


def unit_place(unit):
    if unit < GROUP_DEV:
        return unit, SLOTS - 1
    return (unit - GROUP_DEV) // (SLOTS - 1), (unit - GROUP_DEV) % (SLOTS - 1)


def kernel(
    partner_ref,
    len_ref,
    q_ref,
    k_ref,
    uq_ref,
    ur_ref,
    ab_ref,
    ve_ref,
    tab_ref,
    out_ref,
    xbuf,
    kbuf,
    uq,
    ur,
    ab,
    ve,
    tab,
    front,
    docs,
    recv1_a,
    recv1_b,
    recv1_c,
    snd2,
    recv2_a,
    recv2_b,
    recv2_c,
    final,
    load_sem,
    local_sem,
    own_sem,
    y_send,
    y_recv,
    x_send,
    x_recv,
    t_send,
    t_recv,
    h_send,
    h_recv,
):
    recv1 = (recv1_a, recv1_b, recv1_c)
    recv2 = (recv2_a, recv2_b, recv2_c)
    me_dp = lax.axis_index("dp")
    me_t = lax.axis_index("tensor")
    me_x = me_dp % X_DEV
    me_y = me_dp // X_DEV

    def y_peer(step):
        return lax.rem(me_y + step, Y_DEV) * X_DEV + me_x

    def x_peer(step):
        return me_y * X_DEV + lax.rem(me_x + step, X_DEV)

    def load_units(units, half):
        for unit in units:
            j, s = unit_place(unit)
            rows = pl.ds(j * ROWS + s * DOC, DOC)
            for m in range(MB):
                at = pl.ds(unit * PAIR + m * DOC, DOC)
                pltpu.make_async_copy(q_ref.at[m, rows], xbuf.at[at], load_sem.at[half]).start()
                pltpu.make_async_copy(k_ref.at[m, rows], kbuf.at[at], load_sem.at[2 + half]).start()

    def wait_units(first, count, half):
        at = pl.ds(first * PAIR, count * PAIR)
        pltpu.make_async_copy(xbuf.at[at], xbuf.at[at], load_sem.at[half]).wait()
        pltpu.make_async_copy(kbuf.at[at], kbuf.at[at], load_sem.at[2 + half]).wait()

    weights = ((uq_ref, uq), (ur_ref, ur), (tab_ref, tab), (ab_ref, ab), (ve_ref, ve))

    def weight_copy(n):
        return pltpu.make_async_copy(weights[n][0], weights[n][1], load_sem.at[4 + n])

    weight_copy(0).start()
    load_units(range(BLOCK), 0)
    for n in range(1, 5):
        weight_copy(n).start()
    load_units(range(BLOCK, UNITS), 1)

    barrier = pltpu.get_barrier_semaphore()

    def greet(step, carry):
        pl.semaphore_signal(
            barrier,
            inc=1,
            device_id={"dp": me_dp, "tensor": lax.rem(me_t + step, RANKS)},
            device_id_type=MESH,
        )
        return carry

    lax.fori_loop(1, RANKS, greet, 0)
    for step in range(1, Y_DEV):
        pl.semaphore_signal(
            barrier, inc=1, device_id={"dp": y_peer(step), "tensor": me_t}, device_id_type=MESH
        )
    for step in range(1, X_DEV):
        pl.semaphore_signal(
            barrier, inc=1, device_id={"dp": x_peer(step), "tensor": me_t}, device_id_type=MESH
        )

    scale = (NOPE + ROPE) ** -0.5
    perm_row = lax.broadcasted_iota(jnp.int32, (PAIR, PAIR), 0)
    perm_col = lax.broadcasted_iota(jnp.int32, (PAIR, PAIR), 1)
    perm = (perm_col == (perm_row % MB) * DOC + perm_row // MB).astype(jnp.float32).astype(BF16)
    row_at = lax.broadcasted_iota(jnp.int32, (2 * PAIR, PAIR), 0) % PAIR
    row_micro = row_at % MB
    row_pos = row_at // MB
    key_at = lax.broadcasted_iota(jnp.int32, (2 * PAIR, PAIR), 1)
    key_pos = key_at % DOC
    causal = (key_at // DOC == row_micro) & (key_pos <= row_pos)
    diagonal = key_pos == row_pos
    out_at = lax.broadcasted_iota(jnp.int32, (PAIR, V_HEAD), 0)
    lane = lax.broadcasted_iota(jnp.int32, (PAIR, 128), 1)
    head_lane = [(lane // ROPE == h).astype(jnp.float32).astype(BF16) for h in range(2)]

    def compute(block):
        rows = slice(block * BLOCK * PAIR, (block + 1) * BLOCK * PAIR)
        x = xbuf[rows, :]
        nope = dot(x, uq[...]).astype(BF16)
        rope = dot(x, ur[...])
        mixed_all = [[], []]
        ordered = []
        for i in range(BLOCK):
            at = slice(i * PAIR, (i + 1) * PAIR)
            turned = rotate_pairs(rope[at], tab[0], tab[1]).astype(BF16)
            both = jnp.concatenate([nope[at], turned], 1)
            ordered.append(dot(perm, both).astype(BF16))
        ordered = jnp.concatenate(ordered, 0)
        absorbed = [
            dot(ordered[:, h * NOPE : (h + 1) * NOPE], ab[h * NOPE : (h + 1) * NOPE, :]).astype(BF16)
            for h in range(2)
        ]
        lengths = []
        for i in range(BLOCK):
            unit = block * BLOCK + i
            j, s = unit_place(unit)
            at = slice(i * PAIR, (i + 1) * PAIR)
            here = slice(unit * PAIR, (unit + 1) * PAIR)
            latent = kbuf[here, 0:KV_RANK]
            kr = kbuf[here, KV_RANK : KV_RANK + ROPE].astype(jnp.float32)
            kr = rotate_pairs(jnp.concatenate([kr, kr], 1), tab[0], tab[1]).astype(BF16)
            keys = jnp.concatenate([latent, kr], 1)
            qr = ordered[at, 2 * NOPE :]
            queries = jnp.concatenate(
                [
                    jnp.concatenate([absorbed[h][at], qr * head_lane[h]], 1)
                    for h in range(2)
                ],
                0,
            )
            scores = dot(queries, keys, ((1,), (1,)))
            slot = (me_dp * GROUP_DEV + j) * SLOTS + s
            pair_len = [len_ref[m, slot] for m in range(MB)]
            lengths.append(pair_len)
            live = jnp.where(row_micro == 0, pair_len[0], pair_len[1])
            allowed = causal & ((key_pos < live) | diagonal)
            scores = jnp.where(allowed, scores * scale, -jnp.inf)
            weight = jnp.exp(scores - jnp.max(scores, 1, keepdims=True))
            prob = (weight / jnp.sum(weight, 1, keepdims=True)).astype(BF16)
            mixed = dot(prob, latent).astype(BF16)
            for h in range(2):
                mixed_all[h].append(mixed[h * PAIR : (h + 1) * PAIR])
        for h in range(2):
            res = dot(jnp.concatenate(mixed_all[h], 0), ve[:, h * V_HEAD : (h + 1) * V_HEAD])
            for i in range(BLOCK):
                j, s = unit_place(block * BLOCK + i)
                live = jnp.where(out_at % MB == 0, lengths[i][0], lengths[i][1])
                part = jnp.where(out_at // MB < live, res[i * PAIR : (i + 1) * PAIR], 0.0)
                part = part.astype(BF16)
                if block == 0:
                    docs[j, h] = part
                else:
                    front.at[j, h].reshape((SLOTS - 1) * PAIR, V_HEAD)[
                        s * PAIR : (s + 1) * PAIR, :
                    ] = part

    weight_copy(0).wait()
    weight_copy(1).wait()
    weight_copy(2).wait()
    weight_copy(3).wait()
    weight_copy(4).wait()
    wait_units(0, BLOCK, 0)
    compute(0)

    pl.semaphore_wait(barrier, RANKS - 1 + X_DEV - 1 + Y_DEV - 1)

    def rows_of(c):
        return pl.ds(c * CHUNK, CHUNK)

    def y_copy(step, c):
        return pltpu.make_async_remote_copy(
            src_ref=docs.at[:, :, rows_of(c)],
            dst_ref=recv1[c].at[pl.ds(me_y * GROUP_DEV, GROUP_DEV)],
            send_sem=y_send.at[c, step - 1],
            recv_sem=y_recv.at[c, step - 1],
            device_id={"dp": y_peer(step), "tensor": me_t},
            device_id_type=MESH,
        )

    for c in range(CHUNKS):
        for step in (2, 1, 3):
            y_copy(step, c).start()

    def own_copy(c):
        return pltpu.make_async_copy(
            docs.at[:, :, rows_of(c)],
            recv1[c].at[pl.ds(me_y * GROUP_DEV, GROUP_DEV)],
            own_sem.at[c],
        )

    for c in range(CHUNKS):
        own_copy(c).start()

    wait_units(BLOCK, UNITS - BLOCK, 1)
    for block in range(1, UNITS // BLOCK):
        compute(block)

    mine = pl.ds(me_t * 2, 2)

    def to_rank(rank, source, target, send, recv):
        return pltpu.make_async_remote_copy(
            src_ref=source,
            dst_ref=target,
            send_sem=send.at[rank],
            recv_sem=recv.at[me_t],
            device_id={"dp": me_dp, "tensor": rank},
            device_id_type=MESH,
        )

    def whole(rank, source):
        return to_rank(rank, source, out_ref.at[mine], t_send, t_recv)

    def head_part(rank, source):
        return to_rank(rank, source, out_ref.at[mine, pl.ds(0, HALF)], h_send, h_recv)

    def tail_part(rank, source):
        return to_rank(
            rank, source, out_ref.at[mine, pl.ds(HALF, OWN_ROWS - HALF)], t_send, t_recv
        )

    def front_rows(rank):
        return front.at[rank // SHARE, :, pl.ds(lax.rem(rank, SHARE) * OWN_ROWS, OWN_ROWS)]

    def front_end(rank):
        return front.at[rank // SHARE, :, pl.ds(TAIL, HALF)]

    def final_rows(rank):
        start = (lax.rem(rank, SHARE) - CUT) * OWN_ROWS - HALF
        return final.at[rank // SHARE, :, pl.ds(start, OWN_ROWS)]

    def final_start(rank):
        return final.at[rank // SHARE, :, pl.ds(0, OWN_ROWS - HALF)]

    def send_front(step, carry):
        rank = lax.rem(me_t + step, RANKS)
        place = lax.rem(rank, SHARE)

        @pl.when(place < CUT)
        def _():
            whole(rank, front_rows(rank)).start()

        @pl.when(place == CUT)
        def _():
            head_part(rank, front_end(rank)).start()

        return carry

    lax.fori_loop(1, RANKS, send_front, 0)
    my_place = lax.rem(me_t, SHARE)

    @pl.when(my_place < CUT)
    def _():
        pltpu.make_async_copy(front_rows(me_t), out_ref.at[mine], local_sem.at[1]).start()

    @pl.when(my_place == CUT)
    def _():
        pltpu.make_async_copy(
            front_end(me_t), out_ref.at[mine, pl.ds(0, HALF)], local_sem.at[2]
        ).start()

    even = lax.broadcasted_iota(jnp.int32, (CHUNK, V_HEAD), 0) % MB == 0

    def build(c):
        at = slice(c * CHUNK, (c + 1) * CHUNK)
        for step in range(X_DEV):
            x_at = lax.rem(me_x + step, X_DEV)
            for j in range(GROUP_DEV):
                group = (me_y * X_DEV + x_at) * GROUP_DEV + j
                index = []
                for m in range(MB):
                    mate = partner_ref[m, group]
                    index.append(mate // (X_DEV * GROUP_DEV) * GROUP_DEV + mate % GROUP_DEV)
                for h in range(2):
                    picked = jnp.where(
                        even, recv1[c][index[0], h], recv1[c][index[1], h]
                    )
                    if step == 0:
                        recv2[c][me_x, j, h] = picked
                    else:
                        snd2[step - 1, j, h, at, :] = picked

    def x_copy(step, c):
        return pltpu.make_async_remote_copy(
            src_ref=snd2.at[step - 1, :, :, rows_of(c)],
            dst_ref=recv2[c].at[me_x],
            send_sem=x_send.at[c, step - 1],
            recv_sem=x_recv.at[c, step - 1],
            device_id={"dp": x_peer(step), "tensor": me_t},
            device_id_type=MESH,
        )

    def first_half(c):
        own_copy(c).wait()
        for step in range(1, Y_DEV):
            y_copy(step, c).wait_recv()
        build(c)
        for step in (2, 1, 3):
            x_copy(step, c).start()

    def second_half(c):
        for step in range(1, X_DEV):
            x_copy(step, c).wait_recv()
        at = slice(c * CHUNK // MB, (c + 1) * CHUNK // MB)
        for j in range(GROUP_DEV):
            group = me_dp * GROUP_DEV + j
            source = []
            light = []
            for m in range(MB):
                source.append((partner_ref[m, group] // GROUP_DEV) % X_DEV)
                live = jnp.int32(0)
                for s in range(SLOTS):
                    live += (len_ref[m, group * SLOTS + s] > 0).astype(jnp.int32)
                light.append(live < SLOTS)
            for h in range(2):
                picks = [
                    jnp.where(light[m], recv2[c][source[m], j, h], jnp.zeros((), BF16))
                    for m in range(MB)
                ]
                value = jnp.where(even, picks[0], picks[1])
                final[j, h, at] = value.reshape(CHUNK // MB, MB, V_HEAD)
        low = CUT + 2 * c
        for place in (low, low + 1):

            def send_final(step, carry, place=place):
                rank = lax.rem(me_t // SHARE + step, GROUP_DEV) * SHARE + place

                @pl.when(rank != me_t)
                def _():
                    if place == CUT:
                        tail_part(rank, final_start(rank)).start()
                    else:
                        whole(rank, final_rows(rank)).start()

                return carry

            lax.fori_loop(0, GROUP_DEV, send_final, 0)

    first_half(0)
    first_half(1)
    second_half(0)
    first_half(2)
    second_half(1)
    second_half(2)

    @pl.when(my_place == CUT)
    def _():
        pltpu.make_async_copy(
            final_start(me_t), out_ref.at[mine, pl.ds(HALF, OWN_ROWS - HALF)], local_sem.at[1]
        ).start()

    @pl.when(my_place > CUT)
    def _():
        pltpu.make_async_copy(final_rows(me_t), out_ref.at[mine], local_sem.at[1]).start()

    def await_recv(step, carry):
        source = lax.rem(me_t + step, RANKS)
        theirs = pl.ds(source * 2, 2)

        def arrived(rows, recv):
            part = out_ref.at[theirs, rows]
            pltpu.make_async_copy(part, part, recv.at[source]).wait()

        @pl.when(my_place == CUT)
        def _():
            arrived(pl.ds(0, HALF), h_recv)
            arrived(pl.ds(HALF, OWN_ROWS - HALF), t_recv)

        @pl.when(my_place != CUT)
        def _():
            arrived(pl.ds(0, OWN_ROWS), t_recv)

        return carry

    def await_send(step, carry):
        rank = lax.rem(me_t + step, RANKS)
        place = lax.rem(rank, SHARE)

        @pl.when(place == CUT)
        def _():
            head_part(rank, front_end(rank)).wait_send()
            tail_part(rank, final_start(rank)).wait_send()

        @pl.when(place != CUT)
        def _():
            whole(rank, front.at[0, :, pl.ds(0, OWN_ROWS)]).wait_send()

        return carry

    lax.fori_loop(1, RANKS, await_send, 0)
    for c in range(CHUNKS):
        for step in range(1, Y_DEV):
            y_copy(step, c).wait_send()
        for step in range(1, X_DEV):
            x_copy(step, c).wait_send()

    @pl.when(my_place == CUT)
    def _():
        pltpu.make_async_copy(
            front_end(me_t), out_ref.at[mine, pl.ds(0, HALF)], local_sem.at[2]
        ).wait()
        pltpu.make_async_copy(
            final_start(me_t), out_ref.at[mine, pl.ds(HALF, OWN_ROWS - HALF)], local_sem.at[1]
        ).wait()

    @pl.when(my_place != CUT)
    def _():
        pltpu.make_async_copy(
            front.at[0, :, pl.ds(0, OWN_ROWS)], out_ref.at[mine], local_sem.at[1]
        ).wait()

    lax.fori_loop(1, RANKS, await_recv, 0)


def attend(
    partner, doc_length, query, key, up_query, up_rope, key_absorb, value_expand
):
    smem = pl.BlockSpec(memory_space=pltpu.SMEM)
    anyw = pl.BlockSpec(memory_space=pl.ANY)
    part = (GROUP_DEV, 2, PAIR, V_HEAD)
    return pl.pallas_call(
        kernel,
        out_shape=jax.ShapeDtypeStruct((RANKS * 2, OWN_ROWS, MB, V_HEAD), BF16),
        in_specs=[smem, smem] + [anyw] * 7,
        out_specs=anyw,
        scratch_shapes=[
            pltpu.VMEM((UNITS * PAIR, Q_RANK), BF16),
            pltpu.VMEM((UNITS * PAIR, KV_RANK + ROPE), BF16),
            pltpu.VMEM((Q_RANK, 2 * NOPE), BF16),
            pltpu.VMEM((Q_RANK, 2 * ROPE), BF16),
            pltpu.VMEM((2 * NOPE, KV_RANK), BF16),
            pltpu.VMEM((KV_RANK, 2 * V_HEAD), BF16),
            pltpu.VMEM((2, PAIR, 128), jnp.float32),
            pltpu.VMEM((GROUP_DEV, 2, (SLOTS - 1) * DOC, MB, V_HEAD), BF16),
            pltpu.VMEM(part, BF16),
            *[pltpu.VMEM((Y_DEV * GROUP_DEV, 2, CHUNK, V_HEAD), BF16)] * CHUNKS,
            pltpu.VMEM((X_DEV - 1,) + part, BF16),
            *[pltpu.VMEM((X_DEV, GROUP_DEV, 2, CHUNK, V_HEAD), BF16)] * CHUNKS,
            pltpu.VMEM((GROUP_DEV, 2, DOC, MB, V_HEAD), BF16),
            pltpu.SemaphoreType.DMA((9,)),
            pltpu.SemaphoreType.DMA((3,)),
            pltpu.SemaphoreType.DMA((CHUNKS,)),
            pltpu.SemaphoreType.DMA((CHUNKS, Y_DEV - 1)),
            pltpu.SemaphoreType.DMA((CHUNKS, Y_DEV - 1)),
            pltpu.SemaphoreType.DMA((CHUNKS, X_DEV - 1)),
            pltpu.SemaphoreType.DMA((CHUNKS, X_DEV - 1)),
            pltpu.SemaphoreType.DMA((RANKS,)),
            pltpu.SemaphoreType.DMA((RANKS,)),
            pltpu.SemaphoreType.DMA((RANKS,)),
            pltpu.SemaphoreType.DMA((RANKS,)),
        ],
        compiler_params=pltpu.CompilerParams(collective_id=0, has_side_effects=True),
        name="attend",
    )(
        partner,
        doc_length,
        query,
        key,
        up_query,
        up_rope,
        key_absorb,
        value_expand,
        jnp.asarray(rope_tables()),
    )


def body(
    query_latent, key_latent, partner, doc_length, up_query, up_rope, key_absorb, value_expand
):
    result = attend(
        partner,
        doc_length,
        query_latent,
        key_latent,
        up_query,
        up_rope,
        key_absorb,
        value_expand,
    )
    return result.transpose(2, 1, 0, 3).reshape(MB, OWN_ROWS, RANKS * 2 * V_HEAD)


def solution(mesh):
    in_specs = (
        P(None, "dp", None),
        P(None, "dp", None),
        P(),
        P(),
        P(None, "tensor"),
        P(None, "tensor"),
        P("tensor", None),
        P(None, "tensor"),
    )
    out_specs = P(None, ("dp", "tensor"), None)
    return jax.shard_map(body, mesh=mesh, in_specs=in_specs, out_specs=out_specs, check_vma=False)
```

time: 76.9 us -> 50.7 us (0.66)
  the two profiles are of different devices: /device:TPU:153 before, /device:TPU:8 now
where the time goes in v2:
time: 50.7 us; the launch traced here: 50.5 us
  Pallas kernels  48.4 us (95%)
  local copies, waits for them, and re-layouts  2.12 us (4%)
    pallas_call x1, Pallas kernels, attend(): pl.pallas_call(kernel, out_shape=jax.ShapeDtypeStruct((RANKS * 2, OWN_ROW...  48.4 us
    reshape x1, local copies, waits for them, and re-layouts, body(): result.transpose(2, 1, 0, 3).reshape(MB, OWN_ROWS, RANKS * 2 * V_HEAD)  2.12 us

profile of v2, /device:TPU:8, one launch (start us, length us, event | category | flops | bytes accessed | tf_op | source)
XLA Modules:
  0.0 50.5 jit_solution(10723329627020294998)
XLA Ops:
  0.0 48.4 %attend.1 = bf16[96,9,2,128]{3,2,1,0:T(2,128)(2,1)} custom-call(s32[2,48]{1,0:T(2,128)} %partner_ref.1, s32[2,144]{1,0:T(2,128)} %len_ref.1, bf16[2,432,1536]{2,1,0:T(8,128)(2,1)} %q_ref.1, bf16[2,432,576]{2,1,0:T(8,128)(2,1)} %k_ref.1, bf16[1536,256]{1,0:T(8,128)(2,1)} %uq_ref.1, bf16[1536,128]{1,0:T(8,128)(2,1)} %ur_ref.1, bf16[256,512]{1,0:T(8,128)(2,1)} %ab_ref.1, ...), custom_call_target="tpu_custom_call" | custom-call | tf_op jit(solution)/shard_map/attend/pallas_call | solution.py:502
  48.4 2.1 %copy_bitcast_fusion = bf16[2,9,12288]{2,0,1:T(2,128)(2,1)} fusion(bf16[96,9,2,128]{3,2,1,0:T(2,128)(2,1)} %attend.1), kind=kLoop, calls=%fused_computation | loop fusion | bytes 884736 | tf_op jit(solution)/shard_map/reshape | solution.py:561

commit v3 on v2

--- a/solution.py
+++ b/solution.py
@@ -28,7 +28,8 @@
 CUT = 10
 TAIL = CUT * OWN_ROWS
 HALF = (SLOTS - 1) * DOC - TAIL
-CHUNKS = 3
+CHUNKS = 4
+PLACES = ((CUT, CUT + 1), (CUT + 2,), (CUT + 3,), (CUT + 4, CUT + 5))
 CHUNK = PAIR // CHUNKS
 BF16 = jnp.bfloat16
 
@@ -84,10 +85,12 @@
     recv1_a,
     recv1_b,
     recv1_c,
+    recv1_d,
     snd2,
     recv2_a,
     recv2_b,
     recv2_c,
+    recv2_d,
     final,
     load_sem,
     local_sem,
@@ -101,8 +104,8 @@
     h_send,
     h_recv,
 ):
-    recv1 = (recv1_a, recv1_b, recv1_c)
-    recv2 = (recv2_a, recv2_b, recv2_c)
+    recv1 = (recv1_a, recv1_b, recv1_c, recv1_d)
+    recv2 = (recv2_a, recv2_b, recv2_c, recv2_d)
     me_dp = lax.axis_index("dp")
     me_t = lax.axis_index("tensor")
     me_x = me_dp % X_DEV
@@ -259,9 +262,24 @@
             device_id_type=MESH,
         )
 
-    for c in range(CHUNKS):
-        for step in (2, 1, 3):
-            y_copy(step, c).start()
+    def relay(c):
+        step, back = (1, 3) if c % 2 == 0 else (3, 1)
+        slots = pl.ds(lax.rem(me_y + back, Y_DEV) * GROUP_DEV, GROUP_DEV)
+        return pltpu.make_async_remote_copy(
+            src_ref=recv1[c].at[slots],
+            dst_ref=recv1[c].at[slots],
+            send_sem=y_send.at[c, 1],
+            recv_sem=y_recv.at[c, 1],
+            device_id={"dp": y_peer(step), "tensor": me_t},
+            device_id_type=MESH,
+        )
+
+    def pass_on(c):
+        y_copy(1 if c % 2 == 0 else 3, c).wait_recv()
+        relay(c).start()
+
+    for step, c in ((1, 0), (3, 1), (1, 2), (3, 3), (1, 1), (3, 0), (1, 3), (3, 2)):
+        y_copy(step, c).start()
 
     def own_copy(c):
         return pltpu.make_async_copy(
@@ -274,8 +292,12 @@
         own_copy(c).start()
 
     wait_units(BLOCK, UNITS - BLOCK, 1)
-    for block in range(1, UNITS // BLOCK):
-        compute(block)
+    compute(1)
+    pass_on(0)
+    pass_on(1)
+    compute(2)
+    pass_on(2)
+    pass_on(3)
 
     mine = pl.ds(me_t * 2, 2)
 
@@ -314,7 +336,8 @@
         return final.at[rank // SHARE, :, pl.ds(0, OWN_ROWS - HALF)]
 
     def send_front(step, carry):
-        rank = lax.rem(me_t + step, RANKS)
+        offset = RANKS // 2 + (1 - 2 * (step % 2)) * (step // 2)
+        rank = lax.rem(me_t + offset, RANKS)
         place = lax.rem(rank, SHARE)
 
         @pl.when(place < CUT)
@@ -373,8 +396,8 @@
 
     def first_half(c):
         own_copy(c).wait()
-        for step in range(1, Y_DEV):
-            y_copy(step, c).wait_recv()
+        y_copy(3 if c % 2 == 0 else 1, c).wait_recv()
+        relay(c).wait_recv()
         build(c)
         for step in (2, 1, 3):
             x_copy(step, c).start()
@@ -400,8 +423,7 @@
                 ]
                 value = jnp.where(even, picks[0], picks[1])
                 final[j, h, at] = value.reshape(CHUNK // MB, MB, V_HEAD)
-        low = CUT + 2 * c
-        for place in (low, low + 1):
+        for place in PLACES[c]:
 
             def send_final(step, carry, place=place):
                 rank = lax.rem(me_t // SHARE + step, GROUP_DEV) * SHARE + place
@@ -422,7 +444,9 @@
     second_half(0)
     first_half(2)
     second_half(1)
+    first_half(3)
     second_half(2)
+    second_half(3)
 
     @pl.when(my_place == CUT)
     def _():
@@ -470,8 +494,9 @@
 
     lax.fori_loop(1, RANKS, await_send, 0)
     for c in range(CHUNKS):
-        for step in range(1, Y_DEV):
+        for step in (1, 3):
             y_copy(step, c).wait_send()
+        relay(c).wait_send()
         for step in range(1, X_DEV):
             x_copy(step, c).wait_send()
 

time: 50.7 us -> 48.3 us (0.953)
  the two profiles are of different devices: /device:TPU:8 before, /device:TPU:201 now
where the time goes in v3:
time: 48.3 us; the launch traced here: 48.1 us
  Pallas kernels  46 us (95%)
  local copies, waits for them, and re-layouts  2.12 us (4%)
    pallas_call x1, Pallas kernels, attend(): pl.pallas_call(kernel, out_shape=jax.ShapeDtypeStruct((RANKS * 2, OWN_ROW...  46 us
    reshape x1, local copies, waits for them, and re-layouts, body(): result.transpose(2, 1, 0, 3).reshape(MB, OWN_ROWS, RANKS * 2 * V_HEAD)  2.12 us

profile of v3, /device:TPU:201, one launch (start us, length us, event | category | flops | bytes accessed | tf_op | source)
XLA Modules:
  0.0 48.1 jit_solution(17127730664239216299)
XLA Ops:
  0.0 46.0 %attend.1 = bf16[96,9,2,128]{3,2,1,0:T(2,128)(2,1)} custom-call(s32[2,48]{1,0:T(2,128)} %partner_ref.1, s32[2,144]{1,0:T(2,128)} %len_ref.1, bf16[2,432,1536]{2,1,0:T(8,128)(2,1)} %q_ref.1, bf16[2,432,576]{2,1,0:T(8,128)(2,1)} %k_ref.1, bf16[1536,256]{1,0:T(8,128)(2,1)} %uq_ref.1, bf16[1536,128]{1,0:T(8,128)(2,1)} %ur_ref.1, bf16[256,512]{1,0:T(8,128)(2,1)} %ab_ref.1, ...), custom_call_target="tpu_custom_call" | custom-call | tf_op jit(solution)/shard_map/attend/pallas_call | solution.py:527
  46.0 2.1 %copy_bitcast_fusion = bf16[2,9,12288]{2,0,1:T(2,128)(2,1)} fusion(bf16[96,9,2,128]{3,2,1,0:T(2,128)(2,1)} %attend.1), kind=kLoop, calls=%fused_computation | loop fusion | bytes 884736 | tf_op jit(solution)/shard_map/reshape | solution.py:586

commit v4 on v3

--- a/solution.py
+++ b/solution.py
@@ -426,7 +426,7 @@
         for place in PLACES[c]:
 
             def send_final(step, carry, place=place):
-                rank = lax.rem(me_t // SHARE + step, GROUP_DEV) * SHARE + place
+                rank = lax.rem(me_t // SHARE + 1 + step, GROUP_DEV) * SHARE + place
 
                 @pl.when(rank != me_t)
                 def _():

time: 48.3 us -> 48.4 us (level)
  no operation moved by 1% of the time
where the time goes in v4:
time: 48.4 us; the launch traced here: 48 us
  Pallas kernels  45.9 us (95%)
  local copies, waits for them, and re-layouts  2.12 us (4%)
    pallas_call x1, Pallas kernels, attend(): pl.pallas_call(kernel, out_shape=jax.ShapeDtypeStruct((RANKS * 2, OWN_ROW...  45.9 us
    reshape x1, local copies, waits for them, and re-layouts, body(): result.transpose(2, 1, 0, 3).reshape(MB, OWN_ROWS, RANKS * 2 * V_HEAD)  2.12 us

profile of v4, /device:TPU:201, one launch (start us, length us, event | category | flops | bytes accessed | tf_op | source)
XLA Modules:
  0.0 48.0 jit_solution(681105482759992679)
XLA Ops:
  0.0 45.9 %attend.1 = bf16[96,9,2,128]{3,2,1,0:T(2,128)(2,1)} custom-call(s32[2,48]{1,0:T(2,128)} %partner_ref.1, s32[2,144]{1,0:T(2,128)} %len_ref.1, bf16[2,432,1536]{2,1,0:T(8,128)(2,1)} %q_ref.1, bf16[2,432,576]{2,1,0:T(8,128)(2,1)} %k_ref.1, bf16[1536,256]{1,0:T(8,128)(2,1)} %uq_ref.1, bf16[1536,128]{1,0:T(8,128)(2,1)} %ur_ref.1, bf16[256,512]{1,0:T(8,128)(2,1)} %ab_ref.1, ...), custom_call_target="tpu_custom_call" | custom-call | tf_op jit(solution)/shard_map/attend/pallas_call | solution.py:527
  45.9 2.1 %copy_bitcast_fusion = bf16[2,9,12288]{2,0,1:T(2,128)(2,1)} fusion(bf16[96,9,2,128]{3,2,1,0:T(2,128)(2,1)} %attend.1), kind=kLoop, calls=%fused_computation | loop fusion | bytes 884736 | tf_op jit(solution)/shard_map/reshape | solution.py:586
